TPU v7x, 512 devices: a whole 4x4x16 slice. The times are simulated.
512 devices in a mesh: gx: 64 (over z, x), gy: 8 (over y, core).
Axes of the slice: x: 4, y: 4, z: 16, core: 2. Of those that a mesh axis runs over, the one named last changes fastest.
Arguments:
- velocity: float32 [3, 512, 384, 256], P(None, 'gx', 'gy'), may hold values from -6 to 6
- pressure: float32 [512, 384, 256], P('gx', 'gy'), may hold values from -6 to 6
- viscosity: float32 [512, 384, 256], P('gx', 'gy'), may hold values from 0.12 to 0.6
- wind_profile: float32 [256], replicated, may hold values from 0.5 to 1.5
- panel_area: float32 [16384], P('gy'), may hold values from 0.5 to 2
- slot_cell: int32 [8, 4096], P('gy', 'gx'), may hold values from 0 to 98303
- slot_panel: int32 [8, 4096], P('gy'), may hold values from -1 to 2047, as said below
- panel_shapes: bfloat16 [16384, 2048], P('gy', 'gx'), may hold values from -0.046875 to 0.046875
- node_shapes: bfloat16 [1024, 2048], P(None, 'gx'), may hold values from -0.125 to 0.125
- damper_node: int32 [512], P('gy'), may hold values from 0 to 1022
- damper_viscous: float32 [512], P('gy'), may hold values from 0.2 to 2
- damper_hysteretic: float32 [512], P('gy'), may hold values from 0.2 to 2
- frequency: float32 [2048], P('gx'), may hold values from 0.2 to 1.8
- damping_ratio: float32 [2048], P('gx'), may hold values from 0.05 to 0.5
- modal_state: float32 [2, 2048], P(None, 'gx'), may hold values from -6 to 6
- damper_state: float32 [512], P('gy'), may hold values from -1 to 1
Outputs:
- velocity_next: float32 [3, 512, 384, 256], P(None, 'gx', 'gy')
- pressure_next: float32 [512, 384, 256], P('gx', 'gy')
- modal_next: float32 [2, 2048], P(None, 'gx')
- damper_next: float32 [512], P('gy')
Inputs may be any that keep to these rules, and one draw needn't show every extreme that they name: `slot_panel`: in every row each panel number 0 to 2047 stands in exactly one slot; every other slot holds -1.
All inputs are finite; a program needn't handle non-finite values.
Results may differ from a plain program's by a relative error of at most 0.0013.
Values may be sent and summed in bfloat16 or wider, within the bound.
A program may use at most 64 MiB of HBM per device.

v0:
```python
import jax
import jax.numpy as jnp
from jax import lax
from jax.sharding import PartitionSpec as P

time_step = 0.1
sound_squared = 1.0
modal_step = 0.5
hysteresis_gain = 1.0
shape_beta = 0.5
shape_gamma = 0.5
spring_rate = 0.5


def padded_2(value, sides, width):
    for axis, dim in sides:
        size, length = (lax.axis_size(axis), value.shape[dim])
        up = [(i, (i + 1) % size) for i in range(size - 1)]
        down = [(j, i) for i, j in up]
        last = lax.slice_in_dim(value, length - width, length, axis=dim)
        first = lax.slice_in_dim(value, 0, width, axis=dim)
        before = lax.ppermute(last, axis, up)
        after = lax.ppermute(first, axis, down)
        value = jnp.concatenate([before, value, after], axis=dim)
    return value


def advance(padded, local_viscosity, wind_profile):
    centre_cells = padded[:, 1:-1, 1:-1, 1:-1]
    ahead_cells = padded[:, 2:, 1:-1, 1:-1]
    behind_cells = padded[:, :-2, 1:-1, 1:-1]
    right_cells = padded[:, 1:-1, 2:, 1:-1]
    left_cells = padded[:, 1:-1, :-2, 1:-1]
    above_cells = padded[:, 1:-1, 1:-1, 2:]
    below_cells = padded[:, 1:-1, 1:-1, :-2]
    slope_stream = 0.5 * (ahead_cells - behind_cells)
    slope_span = 0.5 * (right_cells - left_cells)
    slope_vertical = 0.5 * (above_cells - below_cells)
    laplacian = (
        ahead_cells
        + behind_cells
        + right_cells
        + left_cells
        + above_cells
        + below_cells
        - 6.0 * centre_cells
    )
    pressure_slope = jnp.stack([slope_stream[3], slope_span[3], slope_vertical[3]])
    velocity_new = centre_cells[:3] + time_step * (
        -wind_profile * slope_stream[:3] + local_viscosity * laplacian[:3] - pressure_slope
    )
    pressure_new = centre_cells[3] - time_step * sound_squared * (
        slope_stream[0] + slope_span[1] + slope_vertical[2]
    )
    return jnp.concatenate([velocity_new, pressure_new[None]], axis=0)


def vertical_pad(fields):
    return jnp.pad(fields, ((0, 0), (0, 0), (0, 0), (1, 1)))


def body(
    velocity,
    pressure,
    viscosity,
    wind_profile,
    panel_area,
    slot_cell,
    slot_panel,
    panel_shapes,
    node_shapes,
    damper_node,
    damper_viscous,
    damper_hysteretic,
    frequency,
    damping_ratio,
    modal_state,
    damper_state,
):
    fields = jnp.concatenate([velocity, pressure[None]], axis=0)
    for substep in range(2):
        padded = padded_2(fields, (("gx", 1), ("gy", 2)), 1)
        fields = advance(vertical_pad(padded), viscosity, wind_profile)
    velocity_next = fields[:3]
    pressure_next = fields[3]
    slot_count = slot_cell.shape[1]
    panel_count = panel_area.shape[0]
    flat_pressure = pressure_next.reshape(-1)
    sampled = flat_pressure[slot_cell[0]]
    panel_ids = slot_panel[0]
    own_ids = lax.dynamic_slice_in_dim(panel_ids, lax.axis_index("gx") * slot_count, slot_count)
    safe_ids = jnp.where(own_ids < 0, 0, own_ids)
    own_loads = (panel_area[safe_ids] * sampled).astype(jnp.bfloat16)
    every_load = lax.all_gather(own_loads, "gx", axis=0, tiled=True)
    target = jnp.where(panel_ids < 0, panel_count, panel_ids)
    panel_loads = (
        jnp.zeros((panel_count + 1,), jnp.bfloat16).at[target].set(every_load)[:panel_count]
    )
    panel_part = jnp.dot(panel_loads, panel_shapes, preferred_element_type=jnp.float32)
    node_numbers = jnp.arange(node_shapes.shape[0], dtype=jnp.int32)
    upper_pick = (node_numbers[None, :] == damper_node[:, None] + 1).astype(jnp.float32)
    lower_pick = (node_numbers[None, :] == damper_node[:, None]).astype(jnp.float32)
    selector = (upper_pick - lower_pick).astype(jnp.bfloat16)
    drift_shapes = jnp.dot(selector, node_shapes, preferred_element_type=jnp.float32)
    panel_modal = lax.psum(panel_part, "gy")
    displacement = modal_state[0]
    modal_velocity = modal_state[1]
    hysteresis = damper_state
    for modal_turn in range(2):
        stretch, stretch_rate = lax.psum(
            (
                jnp.dot(drift_shapes, displacement, precision=lax.Precision.HIGHEST),
                jnp.dot(drift_shapes, modal_velocity, precision=lax.Precision.HIGHEST),
            ),
            "gx",
        )
        hysteresis = hysteresis + modal_step * (
            hysteresis_gain * stretch_rate
            - shape_beta * jnp.abs(stretch_rate) * hysteresis
            - shape_gamma * stretch_rate * jnp.abs(hysteresis)
        )
        damper_force = -(
            damper_viscous * stretch_rate + spring_rate * stretch + damper_hysteretic * hysteresis
        )
        generalized = jnp.dot(damper_force, drift_shapes, precision=lax.Precision.HIGHEST)
        modal_load = panel_modal + lax.psum(generalized, "gy")
        acceleration = (
            modal_load
            - 2.0 * damping_ratio * frequency * modal_velocity
            - frequency * frequency * displacement
        )
        modal_velocity = modal_velocity + modal_step * acceleration
        displacement = displacement + modal_step * modal_velocity
    return (velocity_next, pressure_next, jnp.stack([displacement, modal_velocity]), hysteresis)


def solution(mesh):
    placed = (
        P(None, "gx", "gy", None),
        P("gx", "gy", None),
        P("gx", "gy", None),
        P(),
        P("gy"),
        P("gy", "gx"),
        P("gy", None),
        P("gy", "gx"),
        P(None, "gx"),
        P("gy"),
        P("gy"),
        P("gy"),
        P("gx"),
        P("gx"),
        P(None, "gx"),
        P("gy"),
    )
    return jax.shard_map(
        body,
        mesh=mesh,
        in_specs=placed,
        out_specs=(P(None, "gx", "gy", None), P("gx", "gy", None), P(None, "gx"), P("gy")),
        check_vma=False,
    )
```

profile of v0, /device:TPU:387, one launch (start us, length us, event | category | flops | bytes accessed | tf_op | source)
XLA Modules:
  0.0 556.4 jit_solution(17609832479686283415)
XLA Ops:
  0.7 1.1 fusion.21
  1.9 3.1 collective-permute-start.1
  5.0 2.2 collective-permute-start
  7.2 0.2 fusion.23
  7.5 0.1 convolution_bitcast_fusion.4
  7.6 0.1 convolution_bitcast_fusion.5
  7.8 1.7 collective-permute-done.1
  9.5 2.8 collective-permute-done
  12.4 5.0 collective-permute-start.3
  17.4 1.9 collective-permute-start.2
  19.3 112.8 %all-reduce.4 = (f32[64]{0:T(128)S(1)}, f32[64]{0:T(128)S(1)}) all-reduce(f32[64]{0:T(128)S(1)} %convolution_bitcast_fusion.4, f32[64]{0:T(128)S(1)} %convolution_bitcast_fusion.5), channel_id=1, replica_groups=mesh['gx'=64,'gy'=8] {'gx'}, use_global_device_ids=true, to_apply=%region_3.4 | all-reduce | flops 128 | bytes 1024 | tf_op jit(solution)/shard_map/psum | solution.py:110
  132.2 3.5 select_maximum_fusion.5
  135.7 0.7 subtract_multiply_fusion.3
  136.4 1.2 subtract_multiply_fusion.5
  137.6 0.2 bitcast_subtract_fusion.1
  137.8 0.9 copy-done.8
  138.7 0.5 copy-done.4
  139.3 1.2 fusion.13
  140.6 3.5 collective-permute-start.5
  144.2 5.2 collective-permute-start.4
  149.5 0.1 convolution_bitcast_fusion.3
  149.6 0.9 collective-permute-done.5
  150.5 1.5 collective-permute-done.4
  152.1 32.2 %collective-permute-start.7 = (f32[4,10,1,256]{3,2,1,0:T(1,128)S(1)}, f32[4,10,1,256]{3,2,1,0:T(1,128)S(1)}, u32[]{:S(2)}, u32[]{:S(2)}) collective-permute-start(f32[4,10,1,256]{3,2,1,0:T(1,128)S(1)} %get-tuple-element.33), channel_id=1, source_target_pairs={{0,1},{1,2},{2,3},{3,4},{4,5},{5,6},{6,7},{8,9},{9,10},{10,11},{11... | collective-permute-start | bytes 122888 | tf_op jit(solution)/shard_map/ppermute | solution.py:22
  184.2 1.9 collective-permute-start.6
  186.2 1.3 dynamic-slice.1
  188.1 0.8 gather_fusion
  188.9 0.7 collective-permute-done.6
  189.5 3.5 select_maximum_fusion
  193.0 2.3 subtract_multiply_fusion
  195.4 0.8 slice.230
  196.1 3.0 subtract_multiply_fusion.2
  199.2 2.4 fusion.17
  201.6 0.7 copy-done.11
  202.3 0.9 copy.20
  203.3 1.8 gather_fusion.1
  205.0 0.2 dynamic-update-slice
  205.3 118.6 %all-reduce.2 = bf16[4096]{0:T(1024)(128)(2,1)S(1)} all-reduce(bf16[4096]{0:T(1024)(128)(2,1)S(1)} %dynamic-update-slice), channel_id=1, replica_groups=mesh['gx'=64,'gy'=8] {'gx'}, use_global_device_ids=true, to_apply=%add.2 | all-reduce | flops 4096 | bytes 16384
  323.9 28.6 %scatter_custom_fusion = bf16[2049]{0:T(1024)(128)(2,1)S(1)} fusion(s32[4096]{0:T(1024)S(1)} %bitcast.100, bf16[4096]{0:T(1024)(128)(2,1)S(1)} %all-reduce.2, bf16[]{:T(256)} %constant.19.clone.1), kind=kCustom, calls=%fused_computation.120 | custom fusion | bytes 4100 | tf_op jit(solution)/shard_map/scatter | solution.py:97
  352.5 0.1 convolution_bitcast_fusion.6
  352.6 39.3 %all-reduce.5 = (f32[32]{0:T(128)S(1)}, f32[32]{0:T(128)S(1)}) all-reduce(f32[32]{0:T(128)S(1)} %convolution_bitcast_fusion.6, f32[32]{0:T(128)S(1)} %convolution_bitcast_fusion.3), channel_id=1, replica_groups=mesh['gx'=64,'gy'=8] {'gy'}, use_global_device_ids=true, to_apply=%region_1.2 | all-reduce | flops 64 | bytes 512 | tf_op jit(solution)/shard_map/psum | solution.py:105
  392.1 0.1 convolution_bitcast_fusion.1
  392.2 1.8 slice.229
  394.0 0.8 slice.228
  394.8 115.8 %all-reduce.3 = (f32[64]{0:T(128)S(1)}, f32[64]{0:T(128)S(1)}) all-reduce(f32[64]{0:T(128)S(1)} %convolution_bitcast_fusion.2, f32[64]{0:T(128)S(1)} %convolution_bitcast_fusion.1), channel_id=1, replica_groups=mesh['gx'=64,'gy'=8] {'gx'}, use_global_device_ids=true, to_apply=%region_5.6 | all-reduce | flops 128 | bytes 1024 | tf_op jit(solution)/shard_map/psum | solution.py:110
  510.8 39.4 %psum.55 = f32[32]{0:T(128)S(1)} all-reduce(f32[32]{0:T(128)S(1)} %convolution_bitcast_fusion), channel_id=1, replica_groups=mesh['gx'=64,'gy'=8] {'gy'}, use_global_device_ids=true, to_apply=%region_7.8 | all-reduce | flops 32 | bytes 256 | tf_op jit(solution)/shard_map/psum | solution.py:126
  550.2 0.6 pad_maximum_fusion.34
  550.8 5.7 %fusion.6 = f32[3,8,48,256]{3,2,1,0:T(8,128)} fusion(f32[3,8,48,256]{3,2,1,0:T(8,128)S(1)} %fusion.13, f32[4,8,48,256]{3,2,1,0:T(8,128)} %get-tuple-element.26, f32[1,8,48,256]{3,2,1,0:T(8,128)S(1)} %get-tuple-element.42, f32[4,8,48,256]{3,2,1,0:T(8,128)} %get-tuple-element.25, f32[4,8,48,256]{3,2,1,0:T(8,128)} %get-tuple-element.31, ...), kind=kLoop, calls=%fused_computation.60 | loop fusion | flops 4718592 | bytes 12583936 | tf_op jit(solution)/shard_map/add | solution.py:49
  (67 shorter events, 0.7 us)
Async XLA Ops:
  0.6 351.8 %copy-start = (bf16[2048,32]{0,1:T(8,128)(2,1)S(1)}, bf16[2048,32]{0,1:T(8,128)(2,1)}, u32[]{:S(2)}) copy-start(bf16[2048,32]{0,1:T(8,128)(2,1)} %param.23) | copy-start | bytes 393220
  0.6 11.7 %copy-start.2 = (f32[3,8,48,256]{3,2,1,0:T(8,128)S(1)}, f32[3,8,48,256]{3,2,1,0:T(8,128)}, u32[]{:S(2)}) copy-start(f32[3,8,48,256]{3,2,1,0:T(8,128)} %param.16) | copy-start | bytes 3538948
  0.7 11.7 %copy-start.3 = (f32[8,48,256]{2,1,0:T(8,128)S(1)}, f32[8,48,256]{2,1,0:T(8,128)}, u32[]{:S(2)}) copy-start(f32[8,48,256]{2,1,0:T(8,128)} %param.17) | copy-start | bytes 1179652
  0.7 6.5 %copy-start.22 = (s32[64]{0:T(128)S(1)}, s32[64]{0:T(128)}, u32[]{:S(2)}) copy-start(s32[64]{0:T(128)} %param.25) | copy-start | bytes 772
  0.7 6.5 %copy-start.21 = (bf16[1024,32]{0,1:T(8,128)(2,1)S(1)}, bf16[1024,32]{0,1:T(8,128)(2,1)}, u32[]{:S(2)}) copy-start(bf16[1024,32]{0,1:T(8,128)(2,1)} %param.24) | copy-start | bytes 196612
  0.7 6.8 %copy-start.12 = (f32[2,32]{1,0:T(2,128)S(1)}, f32[2,32]{1,0:T(2,128)}, u32[]{:S(2)}) copy-start(f32[2,32]{1,0:T(2,128)} %param.30) | copy-start | bytes 772
  0.7 7.0 %copy-start.13 = (s32[1,4096]{1,0:T(1,128)S(1)}, s32[1,4096]{1,0:T(1,128)}, u32[]{:S(2)}) copy-start(s32[1,4096]{1,0:T(1,128)} %param.22) | copy-start | bytes 49156
  0.7 7.1 %copy-start.23 = (s32[1,64]{1,0:T(1,128)S(1)}, s32[1,64]{1,0:T(1,128)}, u32[]{:S(2)}) copy-start(s32[1,64]{1,0:T(1,128)} %param.21) | copy-start | bytes 772
  1.9 17.5 %copy-start.20 = (f32[256]{0:T(256)S(1)}, f32[256]{0:T(256)}, u32[]{:S(2)}) copy-start(f32[256]{0:T(256)} %param.19) | copy-start | bytes 3076
  1.9 7.7 %collective-permute-start.1 = (f32[4,1,48,256]{3,2,1,0:T(8,128)S(1)}, f32[4,1,48,256]{3,2,1,0:T(8,128)S(1)}, u32[]{:S(2)}, u32[]{:S(2)}) collective-permute-start(f32[4,1,48,256]{3,2,1,0:T(8,128)S(1)} %get-tuple-element.46), channel_id=1, source_target_pairs={{0,8},{8,16},{16,24},{24,32},{32,40},{40,48},{48,56},{56,64},{64,7... | collective-permute-start | bytes 589832 | tf_op jit(solution)/shard_map/ppermute | solution.py:22
  5.0 7.3 %collective-permute-start = (f32[4,1,48,256]{3,2,1,0:T(8,128)S(1)}, f32[4,1,48,256]{3,2,1,0:T(8,128)S(1)}, u32[]{:S(2)}, u32[]{:S(2)}) collective-permute-start(f32[4,1,48,256]{3,2,1,0:T(8,128)S(1)} %get-tuple-element.47), channel_id=1, source_target_pairs={{8,0},{16,8},{24,16},{32,24},{40,32},{48,40},{56,48},{64,56},{72,6... | collective-permute-start | bytes 589832 | tf_op jit(solution)/shard_map/ppermute | solution.py:23
  12.4 119.7 %collective-permute-start.3 = (f32[4,10,1,256]{3,2,1,0:T(1,128)S(1)}, f32[4,10,1,256]{3,2,1,0:T(1,128)S(1)}, u32[]{:S(2)}, u32[]{:S(2)}) collective-permute-start(f32[4,10,1,256]{3,2,1,0:T(1,128)S(1)} %get-tuple-element.38), channel_id=1, source_target_pairs={{0,1},{1,2},{2,3},{3,4},{4,5},{5,6},{6,7},{8,9},{9,10},{10,11},{11... | collective-permute-start | bytes 122888 | tf_op jit(solution)/shard_map/ppermute | solution.py:22
  17.4 114.8 %collective-permute-start.2 = (f32[4,10,1,256]{3,2,1,0:T(1,128)S(1)}, f32[4,10,1,256]{3,2,1,0:T(1,128)S(1)}, u32[]{:S(2)}, u32[]{:S(2)}) collective-permute-start(f32[4,10,1,256]{3,2,1,0:T(1,128)S(1)} %get-tuple-element.39), channel_id=1, source_target_pairs={{1,0},{2,1},{3,2},{4,3},{5,4},{6,5},{7,6},{9,8},{10,9},{11,10},{12... | collective-permute-start | bytes 122888 | tf_op jit(solution)/shard_map/ppermute | solution.py:23
  136.4 1.2 copy-start.7
  137.5 1.2 copy-start.8
  137.6 1.7 copy-start.4
  137.6 1.7 copy-start.10
  140.5 9.0 %copy-start.14 = (f32[64]{0:T(128)S(1)}, f32[64]{0:T(128)}, u32[]{:S(2)}) copy-start(f32[64]{0:T(128)} %param.27) | copy-start | bytes 772
  140.5 9.0 %copy-start.15 = (f32[64]{0:T(128)S(1)}, f32[64]{0:T(128)}, u32[]{:S(2)}) copy-start(f32[64]{0:T(128)} %param.26) | copy-start | bytes 772
  140.5 8.9 %copy-start.16 = (f32[64]{0:T(128)S(1)}, f32[64]{0:T(128)}, u32[]{:S(2)}) copy-start(f32[64]{0:T(128)} %param.31) | copy-start | bytes 772
  140.6 47.5 %copy-start.1 = (f32[2048]{0:T(1024)S(1)}, f32[2048]{0:T(1024)}, u32[]{:S(2)}) copy-start(f32[2048]{0:T(1024)} %param.20) | copy-start | bytes 24580
  140.6 9.9 %collective-permute-start.5 = (f32[4,1,48,256]{3,2,1,0:T(8,128)S(1)}, f32[4,1,48,256]{3,2,1,0:T(8,128)S(1)}, u32[]{:S(2)}, u32[]{:S(2)}) collective-permute-start(f32[4,1,48,256]{3,2,1,0:T(8,128)S(1)} %get-tuple-element.40), channel_id=1, source_target_pairs={{0,8},{8,16},{16,24},{24,32},{32,40},{40,48},{48,56},{56,64},{64,7... | collective-permute-start | bytes 589832 | tf_op jit(solution)/shard_map/ppermute | solution.py:22
  144.2 7.8 %collective-permute-start.4 = (f32[4,1,48,256]{3,2,1,0:T(8,128)S(1)}, f32[4,1,48,256]{3,2,1,0:T(8,128)S(1)}, u32[]{:S(2)}, u32[]{:S(2)}) collective-permute-start(f32[4,1,48,256]{3,2,1,0:T(8,128)S(1)} %get-tuple-element.41), channel_id=1, source_target_pairs={{8,0},{16,8},{24,16},{32,24},{40,32},{48,40},{56,48},{64,56},{72,6... | collective-permute-start | bytes 589832 | tf_op jit(solution)/shard_map/ppermute | solution.py:23
  152.1 36.8 %collective-permute-start.7 = (f32[4,10,1,256]{3,2,1,0:T(1,128)S(1)}, f32[4,10,1,256]{3,2,1,0:T(1,128)S(1)}, u32[]{:S(2)}, u32[]{:S(2)}) collective-permute-start(f32[4,10,1,256]{3,2,1,0:T(1,128)S(1)} %get-tuple-element.33), channel_id=1, source_target_pairs={{0,1},{1,2},{2,3},{3,4},{4,5},{5,6},{6,7},{8,9},{9,10},{10,11},{11... | collective-permute-start | bytes 122888 | tf_op jit(solution)/shard_map/ppermute | solution.py:22
  184.2 5.3 collective-permute-start.6
  199.2 2.4 copy-start.5
  199.2 2.4 copy-start.9
  199.2 192.8 %copy-start.18 = (f32[32]{0:T(128)S(1)}, f32[32]{0:T(128)}, u32[]{:S(2)}) copy-start(f32[32]{0:T(128)} %param.28) | copy-start | bytes 388
  199.2 192.8 %copy-start.19 = (f32[32]{0:T(128)S(1)}, f32[32]{0:T(128)}, u32[]{:S(2)}) copy-start(f32[32]{0:T(128)} %param.29) | copy-start | bytes 388
  201.6 0.7 copy-start.11
  202.3 191.7 %copy-start.6 = (f32[4,8,48,256]{3,2,1,0:T(8,128)S(1)}, f32[4,8,48,256]{3,2,1,0:T(8,128)}, u32[]{:S(2)}) copy-start(f32[4,8,48,256]{3,2,1,0:T(8,128)} %copy-done.5) | copy-start | bytes 4718596
  510.6 45.8 %copy-start.17 = (f32[64]{0:T(128)}, f32[64]{0:T(128)S(1)}, u32[]{:S(2)}) copy-start(f32[64]{0:T(128)S(1)} %multiply_add_fusion.1) | copy-start | bytes 772
where the time goes:
time: 557 us; the launch traced here: 556 us
  blocking collectives  426 us (76%)
  starting transfers between devices  55 us (10%)
  local copies, waits for them, and re-layouts  39.3 us (7%)
  other arithmetic  25.7 us (5%)
  waiting for transfers between devices  7.58 us (1%)
    psum x2, blocking collectives, body(): lax.psum((jnp.dot(drift_shapes, displacement, precision=lax.Precision.HIG...  229 us
    unnamed x1, blocking collectives  119 us
    ppermute x4, starting transfers between devices, padded_2(): before = lax.ppermute(last, axis, up)  43.8 us
    psum x1, blocking collectives, body(): modal_load = panel_modal + lax.psum(generalized, 'gy')  39.4 us
    psum x1, blocking collectives, body(): panel_modal = lax.psum(panel_part, 'gy')  39.3 us
    scatter x1, local copies, waits for them, and re-layouts, body(): jnp.zeros((panel_count + 1,), jnp.bfloat16).at[target].set(every_load)  28.6 us
    ppermute x4, starting transfers between devices, padded_2(): after = lax.ppermute(first, axis, down)  11.2 us
  transfers between devices with their start and end apart: 8, of which 5 were waited for; matrix products, arithmetic and copies ran while one was open for 1% of the time, Pallas kernels for 0%

commit v1 on v0

--- a/solution.py
+++ b/solution.py
@@ -1,3 +1,4 @@
+import functools
 import jax
 import jax.numpy as jnp
 from jax import lax
@@ -10,6 +11,13 @@
 shape_beta = 0.5
 shape_gamma = 0.5
 spring_rate = 0.5
+
+
+def scan_teams_here(v0, bus_axis):
+    return jnp.sum(lax.all_gather(v0, axis_name=bus_axis), 0)
+
+
+_fill_threads = functools.partial(scan_teams_here, bus_axis="gy")
 
 
 def padded_2(value, sides, width):
@@ -102,7 +110,7 @@
     lower_pick = (node_numbers[None, :] == damper_node[:, None]).astype(jnp.float32)
     selector = (upper_pick - lower_pick).astype(jnp.bfloat16)
     drift_shapes = jnp.dot(selector, node_shapes, preferred_element_type=jnp.float32)
-    panel_modal = lax.psum(panel_part, "gy")
+    panel_modal = _fill_threads(panel_part)
     displacement = modal_state[0]
     modal_velocity = modal_state[1]
     hysteresis = damper_state

time: 557 us -> 559 us (level)
    unnamed x1 -> x2, blocking collectives: 119 us -> 159 us
    psum x1 -> x0, blocking collectives: 39.3 us -> none  [body(): panel_modal = lax.psum(panel_part, 'gy')]
  transfers between devices with their start and end apart: 8 -> 8, of which waited for: 5 -> 4; matrix products, arithmetic and copies ran while one was open for 1% -> 1% of each run, Pallas kernels for 0% -> 0%
where the time goes in v1:
time: 559 us
  blocking collectives  427 us (76%)
  starting transfers between devices  55 us (10%)
  local copies, waits for them, and re-layouts  40.8 us (7%)
  other arithmetic  25.7 us (5%)
  waiting for transfers between devices  6.93 us (1%)
    psum x2, blocking collectives, body(): lax.psum((jnp.dot(drift_shapes, displacement, precision=lax.Precision.HIG...  229 us
    unnamed x2, blocking collectives  159 us
    ppermute x4, starting transfers between devices, padded_2(): before = lax.ppermute(last, axis, up)  43.8 us
    psum x1, blocking collectives, body(): modal_load = panel_modal + lax.psum(generalized, 'gy')  39.4 us
    scatter x1, local copies, waits for them, and re-layouts, body(): jnp.zeros((panel_count + 1,), jnp.bfloat16).at[target].set(every_load)  28.6 us
    ppermute x4, starting transfers between devices, padded_2(): after = lax.ppermute(first, axis, down)  11.2 us
  transfers between devices with their start and end apart: 8, of which 4 were waited for; matrix products, arithmetic and copies ran while one was open for 1% of the time, Pallas kernels for 0%

profile of v1, /device:TPU:387, one launch (start us, length us, event | category | flops | bytes accessed | tf_op | source)
XLA Modules:
  0.0 558.7 jit_solution(1117556096913941084)
XLA Ops:
  0.7 1.1 fusion.21
  1.9 3.1 collective-permute-start.1
  5.0 2.2 collective-permute-start
  7.2 0.2 fusion.23
  7.6 0.1 convolution_bitcast_fusion.5
  7.8 1.7 collective-permute-done.1
  9.5 2.8 collective-permute-done
  12.4 5.0 collective-permute-start.3
  17.4 1.9 collective-permute-start.2
  19.3 112.8 %all-reduce.5 = (f32[64]{0:T(128)S(1)}, f32[64]{0:T(128)S(1)}) all-reduce(f32[64]{0:T(128)S(1)} %convolution_bitcast_fusion.4, f32[64]{0:T(128)S(1)} %convolution_bitcast_fusion.5), channel_id=1, replica_groups=mesh['gx'=64,'gy'=8] {'gx'}, use_global_device_ids=true, to_apply=%region_3.4 | all-reduce | flops 128 | bytes 1024 | tf_op jit(solution)/shard_map/psum | solution.py:118
  132.2 3.5 select_maximum_fusion.5
  135.7 0.7 subtract_multiply_fusion.3
  136.4 1.2 subtract_multiply_fusion.5
  137.6 0.2 bitcast_subtract_fusion.1
  137.8 0.9 copy-done.8
  138.7 0.5 copy-done.4
  139.3 1.2 fusion.13
  140.6 3.5 collective-permute-start.5
  144.2 5.2 collective-permute-start.4
  149.5 0.1 convolution_bitcast_fusion.3
  149.6 0.9 collective-permute-done.5
  150.5 1.5 collective-permute-done.4
  152.1 32.2 %collective-permute-start.7 = (f32[4,10,1,256]{3,2,1,0:T(1,128)S(1)}, f32[4,10,1,256]{3,2,1,0:T(1,128)S(1)}, u32[]{:S(2)}, u32[]{:S(2)}) collective-permute-start(f32[4,10,1,256]{3,2,1,0:T(1,128)S(1)} %get-tuple-element.33), channel_id=1, source_target_pairs={{0,1},{1,2},{2,3},{3,4},{4,5},{5,6},{6,7},{8,9},{9,10},{10,11},{11... | collective-permute-start | bytes 122888 | tf_op jit(solution)/shard_map/ppermute | solution.py:30
  184.2 1.9 collective-permute-start.6
  186.2 1.3 dynamic-slice.2
  187.4 1.3 dynamic-slice.1
  190.0 0.8 gather_fusion
  190.8 3.5 select_maximum_fusion
  194.3 2.3 subtract_multiply_fusion
  196.6 0.8 slice.230
  197.4 3.0 subtract_multiply_fusion.2
  200.5 2.4 fusion.17
  202.9 0.7 copy-done.11
  203.6 0.9 copy.20
  204.6 1.8 gather_fusion.1
  206.3 0.2 dynamic-update-slice
  206.6 118.3 %all-reduce.2 = bf16[4096]{0:T(1024)(128)(2,1)S(1)} all-reduce(bf16[4096]{0:T(1024)(128)(2,1)S(1)} %dynamic-update-slice), channel_id=1, replica_groups=mesh['gx'=64,'gy'=8] {'gx'}, use_global_device_ids=true, to_apply=%add.2 | all-reduce | flops 4096 | bytes 16384
  324.8 28.6 %scatter_custom_fusion = bf16[2049]{0:T(1024)(128)(2,1)S(1)} fusion(s32[4096]{0:T(1024)S(1)} %bitcast.101, bf16[4096]{0:T(1024)(128)(2,1)S(1)} %all-reduce.2, bf16[]{:T(256)} %constant.19.clone.1), kind=kCustom, calls=%fused_computation.120 | custom fusion | bytes 4100 | tf_op jit(solution)/shard_map/scatter | solution.py:105
  353.4 0.1 convolution_bitcast_fusion.6
  353.6 0.2 dynamic-update-slice.1
  353.8 40.3 %all-reduce.6 = (f32[256]{0:T(256)S(1)}, f32[32]{0:T(128)S(1)}) all-reduce(f32[256]{0:T(256)S(1)} %dynamic-update-slice.1, f32[32]{0:T(128)S(1)} %convolution_bitcast_fusion.3), channel_id=2, replica_groups=mesh['gx'=64,'gy'=8] {'gy'}, use_global_device_ids=true, to_apply=%add.3 | all-reduce | flops 288 | bytes 2304
  394.3 0.1 convolution_bitcast_fusion.1
  394.5 1.8 slice.229
  396.3 0.8 slice.228
  397.0 115.8 %all-reduce.4 = (f32[64]{0:T(128)S(1)}, f32[64]{0:T(128)S(1)}) all-reduce(f32[64]{0:T(128)S(1)} %convolution_bitcast_fusion.2, f32[64]{0:T(128)S(1)} %convolution_bitcast_fusion.1), channel_id=1, replica_groups=mesh['gx'=64,'gy'=8] {'gx'}, use_global_device_ids=true, to_apply=%region_5.6 | all-reduce | flops 128 | bytes 1024 | tf_op jit(solution)/shard_map/psum | solution.py:118
  513.0 39.4 %psum.47 = f32[32]{0:T(128)S(1)} all-reduce(f32[32]{0:T(128)S(1)} %convolution_bitcast_fusion), channel_id=1, replica_groups=mesh['gx'=64,'gy'=8] {'gy'}, use_global_device_ids=true, to_apply=%region_7.8 | all-reduce | flops 32 | bytes 256 | tf_op jit(solution)/shard_map/psum | solution.py:134
  552.4 0.6 pad_maximum_fusion.34
  553.0 5.7 %fusion.6 = f32[3,8,48,256]{3,2,1,0:T(8,128)} fusion(f32[3,8,48,256]{3,2,1,0:T(8,128)S(1)} %fusion.13, f32[4,8,48,256]{3,2,1,0:T(8,128)} %get-tuple-element.26, f32[1,8,48,256]{3,2,1,0:T(8,128)S(1)} %get-tuple-element.42, f32[4,8,48,256]{3,2,1,0:T(8,128)} %get-tuple-element.25, f32[4,8,48,256]{3,2,1,0:T(8,128)} %get-tuple-element.31, ...), kind=kLoop, calls=%fused_computation.60 | loop fusion | flops 4718592 | bytes 12583936 | tf_op jit(solution)/shard_map/add | solution.py:57
  (72 shorter events, 1.0 us)
Async XLA Ops:
  0.6 352.8 %copy-start = (bf16[2048,32]{0,1:T(8,128)(2,1)S(1)}, bf16[2048,32]{0,1:T(8,128)(2,1)}, u32[]{:S(2)}) copy-start(bf16[2048,32]{0,1:T(8,128)(2,1)} %param.23) | copy-start | bytes 393220
  0.6 11.7 %copy-start.2 = (f32[3,8,48,256]{3,2,1,0:T(8,128)S(1)}, f32[3,8,48,256]{3,2,1,0:T(8,128)}, u32[]{:S(2)}) copy-start(f32[3,8,48,256]{3,2,1,0:T(8,128)} %param.16) | copy-start | bytes 3538948
  0.7 11.7 %copy-start.3 = (f32[8,48,256]{2,1,0:T(8,128)S(1)}, f32[8,48,256]{2,1,0:T(8,128)}, u32[]{:S(2)}) copy-start(f32[8,48,256]{2,1,0:T(8,128)} %param.17) | copy-start | bytes 1179652
  0.7 6.5 %copy-start.22 = (s32[64]{0:T(128)S(1)}, s32[64]{0:T(128)}, u32[]{:S(2)}) copy-start(s32[64]{0:T(128)} %param.25) | copy-start | bytes 772
  0.7 6.5 %copy-start.21 = (bf16[1024,32]{0,1:T(8,128)(2,1)S(1)}, bf16[1024,32]{0,1:T(8,128)(2,1)}, u32[]{:S(2)}) copy-start(bf16[1024,32]{0,1:T(8,128)(2,1)} %param.24) | copy-start | bytes 196612
  0.7 6.8 %copy-start.12 = (f32[2,32]{1,0:T(2,128)S(1)}, f32[2,32]{1,0:T(2,128)}, u32[]{:S(2)}) copy-start(f32[2,32]{1,0:T(2,128)} %param.30) | copy-start | bytes 772
  0.7 7.0 %copy-start.13 = (s32[1,4096]{1,0:T(1,128)S(1)}, s32[1,4096]{1,0:T(1,128)}, u32[]{:S(2)}) copy-start(s32[1,4096]{1,0:T(1,128)} %param.22) | copy-start | bytes 49156
  0.7 7.1 %copy-start.23 = (s32[1,64]{1,0:T(1,128)S(1)}, s32[1,64]{1,0:T(1,128)}, u32[]{:S(2)}) copy-start(s32[1,64]{1,0:T(1,128)} %param.21) | copy-start | bytes 772
  1.9 17.5 %copy-start.20 = (f32[256]{0:T(256)S(1)}, f32[256]{0:T(256)}, u32[]{:S(2)}) copy-start(f32[256]{0:T(256)} %param.19) | copy-start | bytes 3076
  1.9 7.7 %collective-permute-start.1 = (f32[4,1,48,256]{3,2,1,0:T(8,128)S(1)}, f32[4,1,48,256]{3,2,1,0:T(8,128)S(1)}, u32[]{:S(2)}, u32[]{:S(2)}) collective-permute-start(f32[4,1,48,256]{3,2,1,0:T(8,128)S(1)} %get-tuple-element.46), channel_id=1, source_target_pairs={{0,8},{8,16},{16,24},{24,32},{32,40},{40,48},{48,56},{56,64},{64,7... | collective-permute-start | bytes 589832 | tf_op jit(solution)/shard_map/ppermute | solution.py:30
  5.0 7.3 %collective-permute-start = (f32[4,1,48,256]{3,2,1,0:T(8,128)S(1)}, f32[4,1,48,256]{3,2,1,0:T(8,128)S(1)}, u32[]{:S(2)}, u32[]{:S(2)}) collective-permute-start(f32[4,1,48,256]{3,2,1,0:T(8,128)S(1)} %get-tuple-element.47), channel_id=1, source_target_pairs={{8,0},{16,8},{24,16},{32,24},{40,32},{48,40},{56,48},{64,56},{72,6... | collective-permute-start | bytes 589832 | tf_op jit(solution)/shard_map/ppermute | solution.py:31
  12.4 119.7 %collective-permute-start.3 = (f32[4,10,1,256]{3,2,1,0:T(1,128)S(1)}, f32[4,10,1,256]{3,2,1,0:T(1,128)S(1)}, u32[]{:S(2)}, u32[]{:S(2)}) collective-permute-start(f32[4,10,1,256]{3,2,1,0:T(1,128)S(1)} %get-tuple-element.38), channel_id=1, source_target_pairs={{0,1},{1,2},{2,3},{3,4},{4,5},{5,6},{6,7},{8,9},{9,10},{10,11},{11... | collective-permute-start | bytes 122888 | tf_op jit(solution)/shard_map/ppermute | solution.py:30
  17.4 114.8 %collective-permute-start.2 = (f32[4,10,1,256]{3,2,1,0:T(1,128)S(1)}, f32[4,10,1,256]{3,2,1,0:T(1,128)S(1)}, u32[]{:S(2)}, u32[]{:S(2)}) collective-permute-start(f32[4,10,1,256]{3,2,1,0:T(1,128)S(1)} %get-tuple-element.39), channel_id=1, source_target_pairs={{1,0},{2,1},{3,2},{4,3},{5,4},{6,5},{7,6},{9,8},{10,9},{11,10},{12... | collective-permute-start | bytes 122888 | tf_op jit(solution)/shard_map/ppermute | solution.py:31
  136.4 1.2 copy-start.7
  137.5 1.2 copy-start.8
  137.6 1.7 copy-start.4
  137.6 1.7 copy-start.10
  140.5 9.0 %copy-start.14 = (f32[64]{0:T(128)S(1)}, f32[64]{0:T(128)}, u32[]{:S(2)}) copy-start(f32[64]{0:T(128)} %param.27) | copy-start | bytes 772
  140.5 9.0 %copy-start.15 = (f32[64]{0:T(128)S(1)}, f32[64]{0:T(128)}, u32[]{:S(2)}) copy-start(f32[64]{0:T(128)} %param.26) | copy-start | bytes 772
  140.5 8.9 %copy-start.16 = (f32[64]{0:T(128)S(1)}, f32[64]{0:T(128)}, u32[]{:S(2)}) copy-start(f32[64]{0:T(128)} %param.31) | copy-start | bytes 772
  140.6 49.4 %copy-start.1 = (f32[2048]{0:T(1024)S(1)}, f32[2048]{0:T(1024)}, u32[]{:S(2)}) copy-start(f32[2048]{0:T(1024)} %param.20) | copy-start | bytes 24580
  140.6 9.9 %collective-permute-start.5 = (f32[4,1,48,256]{3,2,1,0:T(8,128)S(1)}, f32[4,1,48,256]{3,2,1,0:T(8,128)S(1)}, u32[]{:S(2)}, u32[]{:S(2)}) collective-permute-start(f32[4,1,48,256]{3,2,1,0:T(8,128)S(1)} %get-tuple-element.40), channel_id=1, source_target_pairs={{0,8},{8,16},{16,24},{24,32},{32,40},{40,48},{48,56},{56,64},{64,7... | collective-permute-start | bytes 589832 | tf_op jit(solution)/shard_map/ppermute | solution.py:30
  144.2 7.8 %collective-permute-start.4 = (f32[4,1,48,256]{3,2,1,0:T(8,128)S(1)}, f32[4,1,48,256]{3,2,1,0:T(8,128)S(1)}, u32[]{:S(2)}, u32[]{:S(2)}) collective-permute-start(f32[4,1,48,256]{3,2,1,0:T(8,128)S(1)} %get-tuple-element.41), channel_id=1, source_target_pairs={{8,0},{16,8},{24,16},{32,24},{40,32},{48,40},{56,48},{64,56},{72,6... | collective-permute-start | bytes 589832 | tf_op jit(solution)/shard_map/ppermute | solution.py:31
  152.1 38.7 %collective-permute-start.7 = (f32[4,10,1,256]{3,2,1,0:T(1,128)S(1)}, f32[4,10,1,256]{3,2,1,0:T(1,128)S(1)}, u32[]{:S(2)}, u32[]{:S(2)}) collective-permute-start(f32[4,10,1,256]{3,2,1,0:T(1,128)S(1)} %get-tuple-element.33), channel_id=1, source_target_pairs={{0,1},{1,2},{2,3},{3,4},{4,5},{5,6},{6,7},{8,9},{9,10},{10,11},{11... | collective-permute-start | bytes 122888 | tf_op jit(solution)/shard_map/ppermute | solution.py:30
  184.2 6.6 %collective-permute-start.6 = (f32[4,10,1,256]{3,2,1,0:T(1,128)S(1)}, f32[4,10,1,256]{3,2,1,0:T(1,128)S(1)}, u32[]{:S(2)}, u32[]{:S(2)}) collective-permute-start(f32[4,10,1,256]{3,2,1,0:T(1,128)S(1)} %get-tuple-element.34), channel_id=1, source_target_pairs={{1,0},{2,1},{3,2},{4,3},{5,4},{6,5},{7,6},{9,8},{10,9},{11,10},{12... | collective-permute-start | bytes 122888 | tf_op jit(solution)/shard_map/ppermute | solution.py:31
  200.5 2.4 copy-start.5
  200.5 2.4 copy-start.9
  200.5 193.7 %copy-start.18 = (f32[32]{0:T(128)S(1)}, f32[32]{0:T(128)}, u32[]{:S(2)}) copy-start(f32[32]{0:T(128)} %param.28) | copy-start | bytes 388
  200.5 193.7 %copy-start.19 = (f32[32]{0:T(128)S(1)}, f32[32]{0:T(128)}, u32[]{:S(2)}) copy-start(f32[32]{0:T(128)} %param.29) | copy-start | bytes 388
  202.9 0.7 copy-start.11
  203.6 192.7 %copy-start.6 = (f32[4,8,48,256]{3,2,1,0:T(8,128)S(1)}, f32[4,8,48,256]{3,2,1,0:T(8,128)}, u32[]{:S(2)}) copy-start(f32[4,8,48,256]{3,2,1,0:T(8,128)} %copy-done.5) | copy-start | bytes 4718596
  512.8 45.8 %copy-start.17 = (f32[64]{0:T(128)}, f32[64]{0:T(128)S(1)}, u32[]{:S(2)}) copy-start(f32[64]{0:T(128)S(1)} %multiply_add_fusion.1) | copy-start | bytes 772
